TPU v7x, 32 devices: a whole 2x2x4 slice. The times are simulated.
32 devices in a mesh: row: 8 (over z, core), col: 4 (over y, x).
Axes of the slice: x: 2, y: 2, z: 4, core: 2. Of those that a mesh axis runs over, the one named last changes fastest.
Arguments:
- pair_elems: bfloat16 [320, 12288], P('row', 'col'), may hold values from -0.59765625 to 0.59765625
- counts: int32 [8], replicated, may hold values from 1 to 40, 200 in all
- val_band: int32 [320], replicated, may hold values from 0 to 127
- cond_band: int32 [320], replicated, may hold values from 0 to 511
- val_energy: float32 [128], replicated, may hold values from -12 to -0.5
- cond_energy: float32 [512], replicated, may hold values from 0.5 to 12
- frequency: float32 [3], replicated, may hold values from 0.3 to 6
Outputs:
- chi: float32 [3, 12288, 12288], P(None, 'row', 'col')
Inputs may be any that keep to these rules, and one draw needn't show every extreme that they name: counts sum to 200, and the largest is 40.
All inputs are finite; a program needn't handle non-finite values.
Results may differ from a plain program's by a relative error of at most 0.0028.
Values may be sent and summed in bfloat16 or wider, within the bound.
A program may use at most 128 MiB of HBM per device.

v0:
```python
import jax
import jax.numpy as jnp
from jax import lax
from jax.sharding import PartitionSpec as P


def broadcast(x, axis, root):
    mine = lax.axis_index(axis) == root
    return lax.psum(jnp.where(mine, x, jnp.zeros_like(x)), axis)


def lookup_energy(band, table):
    levels = jnp.arange(table.shape[0], dtype=jnp.int32)
    return jnp.sum(jnp.where(band[:, None] == levels[None, :], table[None, :], 0.0), axis=1)


def per_device(pair_elems, counts, val_band, cond_band, val_energy, cond_energy, frequency):
    capacity = pair_elems.shape[0]
    col_width = pair_elems.shape[1]
    row_count = lax.axis_size("row")
    col_count = lax.axis_size("col")
    plane_waves = col_width * col_count
    row_width = plane_waves // row_count
    slot_count = row_count * capacity
    position = jnp.arange(slot_count, dtype=jnp.int32)
    limits = jnp.repeat(counts, capacity)
    live_mask = (position % capacity < limits).astype(jnp.float32)
    energy_gap = lookup_energy(cond_band, cond_energy) - lookup_energy(val_band, val_energy)
    weights = (
        -4.0
        * live_mask[None, :]
        * energy_gap[None, :]
        / (energy_gap[None, :] ** 2 + frequency[:, None] ** 2)
    )
    row_index = lax.axis_index("row")
    columns = lax.all_gather(pair_elems, "row", axis=0, tiled=True)
    offset = row_index * row_width % col_width
    segment = lax.dynamic_slice_in_dim(columns, offset, row_width, 1)
    row_operand = broadcast(segment, "col", row_index * row_width // col_width)
    row_float = row_operand.astype(jnp.float32)
    freq_count = weights.shape[0]
    dims = (((0,), (0,)), ((), ()))
    scaled = jnp.concatenate(
        [(row_float * weights[which][:, None]).astype(jnp.bfloat16) for which in range(freq_count)],
        axis=1,
    )
    product = lax.dot_general(scaled, columns, dims, preferred_element_type=jnp.float32)
    return product.reshape(freq_count, row_width, col_width)


def solution(mesh):
    in_specs = (P("row", "col"), P(), P(), P(), P(), P(), P())
    out_specs = P(None, "row", "col")
    return jax.shard_map(
        per_device, mesh=mesh, in_specs=in_specs, out_specs=out_specs, check_vma=False
    )
```

profile of v0, /device:TPU:3, one launch (start us, length us, event | category | flops | bytes accessed | tf_op | source)
XLA Modules:
  0.0 123.9 jit_solution(12927003484726928838)
XLA Ops:
  6.5 0.0 copy-start.6
  6.5 0.0 copy-start.4
  6.5 0.0 copy-start.2
  6.6 0.0 all-gather.2.cloned.1.call-start
  6.6 0.7 all-gather.2.cloned.1.call-update
  7.3 0.0 all-reduce.2.cloned.1.call-start
  7.4 31.3 %all-gather.2.cloned.1.call-done = bf16[320,3072]{1,0:T(8,128)(2,1)} async-done(((bf16[40,3072]{1,0:T(8,128)(2,1)}), bf16[320,3072]{1,0:T(8,128)(2,1)}) %all-gather.2.cloned.1.call-update) | async-done | bytes 1966096 | tf_op jit(solution)/shard_map/all_gather | solution.py:36
  38.7 2.6 %dynamic-slice_select_fusion = bf16[320,1536]{1,0:T(8,128)(2,1)} fusion(bf16[320,3072]{1,0:T(8,128)(2,1)} %all-gather.2.cloned.1.call-done, s32[]{:T(128)S(6)} %select_n.43, pred[]{:T(512)S(6)} %eq.18), kind=kLoop, calls=%fused_computation.12 | loop fusion | flops 491520 | bytes 1966085 | tf_op jit(solution)/shard_map/jit(_where)/select_n | solution.py:9
  41.3 0.0 all-reduce.2.cloned.1.call-update
  41.4 0.0 copy-done.6
  41.4 0.0 copy-done.4
  41.4 0.1 broadcast_in_dim.41
  41.5 0.1 reshape.44
  41.5 0.0 copy-done.5
  41.5 0.0 copy-done.3
  41.6 0.2 select_reduce_fusion.1
  41.8 0.0 copy-done.1
  41.8 0.0 copy-done.2
  41.8 0.2 select_reduce_fusion
  42.0 0.1 add_divide_fusion
  42.1 50.1 %all-reduce.2.cloned.1.call-done = bf16[320,1536]{1,0:T(8,128)(2,1)} async-done(((bf16[320,1536]{1,0:T(8,128)(2,1)}), bf16[320,1536]{1,0:T(8,128)(2,1)}) %all-reduce.2.cloned.1.call-update) | async-done | bytes 983056 | tf_op jit(solution)/shard_map/psum | solution.py:9
  92.2 1.6 %fusion.6 = (bf16[320,1536]{1,0:T(8,128)(2,1)S(1)}, bf16[320,1536]{1,0:T(8,128)(2,1)S(1)}, bf16[320,1536]{1,0:T(8,128)(2,1)S(1)}) fusion(bf16[320,1536]{1,0:T(8,128)(2,1)} %all-reduce.2.cloned.1.call-done, f32[320]{0:T(512)S(1)} %get-tuple-element.5, f32[320]{0:T(512)S(1)} %get-tuple-element.7, f32[320]{0:T(512)S(1)} %get-tuple-element.6), kind=kLoop, calls=%fused_computation.9 | loop fusion | flops 3440640 | bytes 3936000 | tf_op jit(solution)/shard_map/convert_element_type | solution.py:44
  93.9 0.0 copy-done
  93.9 23.2 %fusion = f32[4608,3072]{1,0:T(8,128)} fusion(bf16[320,3072]{1,0:T(8,128)(2,1)S(1)} %copy-done, bf16[320,1536]{1,0:T(8,128)(2,1)S(1)} %get-tuple-element.10, bf16[320,1536]{1,0:T(8,128)(2,1)S(1)} %get-tuple-element.9, bf16[320,1536]{1,0:T(8,128)(2,1)S(1)} %get-tuple-element.8), kind=kOutput, calls=%fused_computation | convolution fusion | flops 9068544000 | bytes 61538304 | tf_op jit(solution)/shard_map/dot_general | solution.py:47
  (7 shorter events, 0.1 us)
Async XLA Ops:
  6.5 34.8 %copy-start.6 = (f32[3]{0:T(128)S(1)}, f32[3]{0:T(128)}, u32[]{:S(2)}) copy-start(f32[3]{0:T(128)} %param.13) | copy-start | bytes 40
  6.5 34.8 %copy-start.4 = (s32[8]{0:T(128)S(1)}, s32[8]{0:T(128)}, u32[]{:S(2)}) copy-start(s32[8]{0:T(128)} %param.8) | copy-start | bytes 100
  6.5 35.0 %copy-start.5 = (f32[128]{0:T(128)S(1)}, f32[128]{0:T(128)}, u32[]{:S(2)}) copy-start(f32[128]{0:T(128)} %param.11) | copy-start | bytes 1540
  6.5 35.0 %copy-start.3 = (s32[320]{0:T(512)S(1)}, s32[320]{0:T(512)}, u32[]{:S(2)}) copy-start(s32[320]{0:T(512)} %param.9) | copy-start | bytes 3844
  6.5 35.2 %copy-start.1 = (f32[512]{0:T(512)S(1)}, f32[512]{0:T(512)}, u32[]{:S(2)}) copy-start(f32[512]{0:T(512)} %param.12) | copy-start | bytes 6148
  6.5 35.2 %copy-start.2 = (s32[320]{0:T(512)S(1)}, s32[320]{0:T(512)}, u32[]{:S(2)}) copy-start(s32[320]{0:T(512)} %param.10) | copy-start | bytes 3844
  6.6 32.2 %all-gather.2.cloned.1.call-start = ((), (), s32[]{:S(2)}) async-start(), calls=%async_computation | async-start | bytes 2211840 | tf_op jit(solution)/shard_map/all_gather | solution.py:36
  7.3 84.9 %all-reduce.2.cloned.1.call-start = ((), (), s32[]{:S(2)}) async-start(), calls=%async_computation.1 | async-start | bytes 1966080 | tf_op jit(solution)/shard_map/psum | solution.py:9
  41.3 52.5 %copy-start = (bf16[320,3072]{1,0:T(8,128)(2,1)S(1)}, bf16[320,3072]{1,0:T(8,128)(2,1)}, u32[]{:S(2)}) copy-start(bf16[320,3072]{1,0:T(8,128)(2,1)} %all-gather.2.cloned.1.call-done) | copy-start | bytes 5898244
Sparse Core Ops, SparseCore 0:
  9.0 29.6 all-gather.1
  41.9 50.3 all-reduce.1
where the time goes:
time: 126 us; the launch traced here: 124 us
  waiting for transfers between devices  82.1 us (65%)
  matrix products  23.2 us (18%)
  between operations  13.5 us (11%)
  other arithmetic  4.77 us (4%)
    psum x1, waiting for transfers between devices, broadcast(): return lax.psum(jnp.where(mine, x, jnp.zeros_like(x)), axis)  50.1 us
    all_gather x1, waiting for transfers between devices, per_device(): columns = lax.all_gather(pair_elems, 'row', axis=0, tiled=True)  31.3 us
    dot_general x1, matrix products, per_device(): lax.dot_general(scaled, columns, dims, preferred_element_type=jnp.float32)  23.2 us
    select_n x1, other arithmetic, broadcast(): return lax.psum(jnp.where(mine, x, jnp.zeros_like(x)), axis)  2.61 us
  transfers between devices with their start and end apart: 2, of which 2 were waited for; matrix products, arithmetic and copies ran while one was open for 1% of the time, Pallas kernels for 0%

commit v1 on v0

v1 whole, which is shorter than its diff:
```python
import functools

import jax
import jax.numpy as jnp
from jax import lax
from jax.experimental import pallas as pl
from jax.experimental.pallas import tpu as pltpu
from jax.sharding import PartitionSpec as P

MESH = pl.DeviceIdType.MESH
LAG = 2


def ring_place(c, count):
    if count == 4:
        return c + (c // 2) * (1 - 2 * (c % 2))
    return c


def gather_kernel(rows, cols, halves, x_ref, cols_ref, seg_ref, own_sem, line_send, line_recv, mate_send, mate_recv,
                  enter_send, relay_send, ring_recv):
    r, c = lax.axis_index("row"), lax.axis_index("col")
    chips = rows // 2
    q, k = r // 2, r % 2
    width = x_ref.shape[1]
    ratio = rows // cols
    seg_width = width // ratio
    chunk = seg_width // halves
    chunks = ratio * halves
    lane = chunk // 2
    place = ring_place(c, cols)
    source = r // ratio
    ring_next = [ring_place((place + 1) % cols, cols), ring_place((place + cols - 1) % cols, cols)]
    up_ok, down_ok = q + 1 < chips, q >= 1

    own = pltpu.make_async_copy(x_ref, cols_ref.at[r], own_sem)
    own.start()
    barrier = pltpu.get_barrier_semaphore()

    def greet(row, col):
        pl.semaphore_signal(barrier, inc=1, device_id=(row, col), device_id_type=MESH)

    mate = 2 * q + 1 - k
    greet(mate, c)
    for nxt in ring_next:
        greet(2 * q, nxt)
        greet(2 * q + 1, nxt)

    @pl.when(up_ok)
    def _():
        greet(r + 2, c)

    @pl.when(down_ok)
    def _():
        greet(r - 2, c)

    pl.semaphore_wait(barrier, 5 + up_ok.astype(jnp.int32) + down_ok.astype(jnp.int32))
    own.wait()

    def remote(src, dst, send, recv, row, col):
        return pltpu.make_async_remote_copy(
            src_ref=src, dst_ref=dst, send_sem=send, recv_sem=recv, device_id=(row, col), device_id_type=MESH
        )

    def span(start, size):
        return pl.ds(pl.multiple_of(start, 128), size)

    def block_of(stream, d, core):
        return 2 * (q - d if stream == 0 else q + d) + core

    def has(stream, d):
        return q >= d if stream == 0 else q + d < chips

    def line_copy(stream, d, j, b):
        ref = cols_ref.at[b, :, span(j * chunk, chunk)]
        row = r + 2 if stream == 0 else r - 2
        return remote(ref, ref, line_send.at[stream, d, j], line_recv.at[stream, d, j], row, c)

    def line_arrival(stream, d, j, b):
        ref = cols_ref.at[b, :, span(j * chunk, chunk)]
        return remote(ref, ref, line_send.at[stream, d, j], line_recv.at[stream, d - 1, j], mate, c)

    def mate_copy(b, j):
        ref = cols_ref.at[b, :, span(j * chunk, chunk)]
        return remote(ref, ref, mate_send.at[b, j], mate_recv.at[b, j], mate, c)

    def enter_copy(b, j, way):
        g = c * ratio + j // halves
        src = cols_ref.at[b, :, span(j * chunk + way * lane, lane)]
        dst = seg_ref.at[b, :, span((j % halves) * chunk + way * lane, lane)]
        return remote(src, dst, enter_send.at[b, j, way], ring_recv.at[b, j % halves, way], g, ring_next[way])

    def relay_copy(b, j, way):
        ref = seg_ref.at[b, :, span((j % halves) * chunk + way * lane, lane)]
        return remote(ref, ref, relay_send.at[b, j % halves, way], ring_recv.at[b, j % halves, way], r, ring_next[way])

    def feeds(j):
        return (c * ratio + j // halves) // 2 == q

    def relays(j):
        return (source != c) & (j // halves == r % ratio)

    def onward(stream):
        return up_ok if stream == 0 else down_ok

    def line_part(step):
        j, d = step // chips, step % chips
        for stream in (0, 1):
            here = has(stream, d) if stream == 0 else has(stream, d) & (d > 0)
            b = block_of(stream, d, k)

            @pl.when(has(stream, d))
            def _():
                @pl.when(d > 0)
                def _():
                    line_arrival(stream, d, j, b).wait_recv()

                @pl.when(onward(stream))
                def _():
                    line_copy(stream, d, j, b).start()

            @pl.when(here)
            def _():
                mate_copy(b, j).start()

                @pl.when(feeds(j))
                def _():
                    for way in (0, 1):
                        enter_copy(b, j, way).start()

    def ring_part(step):
        j, d = step // chips, step % chips

        @pl.when(relays(j))
        def _():
            for stream in (0, 1):
                here = has(stream, d) if stream == 0 else has(stream, d) & (d > 0)

                @pl.when(here)
                def _():
                    for core in (0, 1):
                        b = block_of(stream, d, core)
                        for way in (0, 1):
                            relay_copy(b, j, way).wait_recv()

                            @pl.when(ring_next[way] != source)
                            def _():
                                relay_copy(b, j, way).start()

    steps = chunks * chips

    def body(step, carry):
        @pl.when(step < steps)
        def _():
            line_part(step)

        @pl.when(step >= LAG)
        def _():
            ring_part(step - LAG)

        return carry

    lax.fori_loop(0, steps + LAG, body, 0)

    def finish(step, carry):
        j, d = step // chips, step % chips
        for stream in (0, 1):
            here = has(stream, d) if stream == 0 else has(stream, d) & (d > 0)
            b = block_of(stream, d, k)
            theirs = block_of(stream, d, 1 - k)

            @pl.when(has(stream, d) & onward(stream))
            def _():
                line_copy(stream, d, j, b).wait_send()

            @pl.when(here)
            def _():
                mate_copy(b, j).wait_send()
                mate_copy(theirs, j).wait_recv()

                @pl.when(feeds(j))
                def _():
                    for way in (0, 1):
                        enter_copy(b, j, way).wait_send()

                @pl.when(relays(j))
                def _():
                    for core in (0, 1):
                        e = block_of(stream, d, core)
                        for way in (0, 1):
                            @pl.when(ring_next[way] != source)
                            def _():
                                relay_copy(e, j, way).wait_send()

        return carry

    lax.fori_loop(0, steps, finish, 0)

    @pl.when(source == c)
    def _():
        here = pltpu.make_async_copy(cols_ref.at[:, :, span((r % ratio) * seg_width, seg_width)], seg_ref, own_sem)
        here.start()
        here.wait()


def gather(x, rows, cols):
    capacity, width = x.shape
    ratio = rows // cols
    seg_width = width // ratio
    halves = 2 if seg_width % 512 == 0 else 1
    chunks, chips = ratio * halves, rows // 2
    dma = pltpu.SemaphoreType.DMA
    return pl.pallas_call(
        functools.partial(gather_kernel, rows, cols, halves),
        out_shape=(
            jax.ShapeDtypeStruct((rows, capacity, width), x.dtype),
            jax.ShapeDtypeStruct((rows, capacity, seg_width), x.dtype),
        ),
        in_specs=[pl.BlockSpec(memory_space=pl.ANY)],
        out_specs=(pl.BlockSpec(memory_space=pltpu.VMEM), pl.BlockSpec(memory_space=pltpu.VMEM)),
        scratch_shapes=[
            dma,
            dma((2, chips, chunks)),
            dma((2, chips, chunks)),
            dma((rows, chunks)),
            dma((rows, chunks)),
            dma((rows, chunks, 2)),
            dma((rows, halves, 2)),
            dma((rows, halves, 2)),
        ],
        compiler_params=pltpu.CompilerParams(collective_id=0, has_side_effects=True),
    )(x)


def product_kernel(weights_ref, seg_ref, cols_ref, out_ref):
    which = pl.program_id(1)
    slots, width = weights_ref.shape[1], cols_ref.shape[2]
    weight = weights_ref[which]
    seg = seg_ref[...].reshape(slots, seg_ref.shape[2]).astype(jnp.float32)
    scaled = (seg * weight).astype(jnp.bfloat16)
    columns = cols_ref[...].reshape(slots, width)
    out_ref[0] = lax.dot_general(
        scaled, columns, (((0,), (0,)), ((), ())), preferred_element_type=jnp.float32
    )


def product(weights, seg, columns):
    freqs = weights.shape[0]
    rows, capacity, seg_width = seg.shape
    width = columns.shape[2]
    slots = rows * capacity
    tile = 256
    return pl.pallas_call(
        product_kernel,
        out_shape=jax.ShapeDtypeStruct((freqs, seg_width, width), jnp.float32),
        grid=(seg_width // tile, freqs),
        in_specs=[
            pl.BlockSpec((freqs, slots, 1), lambda m, f: (0, 0, 0), pipeline_mode=pl.Buffered(1)),
            pl.BlockSpec((rows, capacity, tile), lambda m, f: (0, 0, m)),
            pl.BlockSpec((rows, capacity, width), lambda m, f: (0, 0, 0), pipeline_mode=pl.Buffered(1)),
        ],
        out_specs=pl.BlockSpec((1, tile, width), lambda m, f: (f, m, 0)),
        compiler_params=pltpu.CompilerParams(vmem_limit_bytes=48 * 1024 * 1024),
    )(weights[:, :, None], seg, columns)


def lookup_energy(band, table):
    levels = jnp.arange(table.shape[0], dtype=jnp.int32)
    return jnp.sum(jnp.where(band[:, None] == levels[None, :], table[None, :], 0.0), axis=1)


def per_device(pair_elems, counts, val_band, cond_band, val_energy, cond_energy, frequency):
    capacity = pair_elems.shape[0]
    rows, cols = lax.axis_size("row"), lax.axis_size("col")
    position = jnp.arange(rows * capacity, dtype=jnp.int32)
    limits = jnp.repeat(counts, capacity)
    live_mask = (position % capacity < limits).astype(jnp.float32)
    energy_gap = lookup_energy(cond_band, cond_energy) - lookup_energy(val_band, val_energy)
    weights = (
        -4.0
        * live_mask[None, :]
        * energy_gap[None, :]
        / (energy_gap[None, :] ** 2 + frequency[:, None] ** 2)
    )
    columns, seg = gather(pair_elems, rows, cols)
    return product(weights, seg, columns)


def solution(mesh):
    in_specs = (P("row", "col"), P(), P(), P(), P(), P(), P())
    out_specs = P(None, "row", "col")
    return jax.shard_map(
        per_device, mesh=mesh, in_specs=in_specs, out_specs=out_specs, check_vma=False
    )
```

time: 126 us -> 330 us (2.62)
  Pallas kernels: 0 us -> 323 us
  waiting for transfers between devices: 82.1 us -> 0 us
  matrix products: 23.2 us -> 0 us
  between operations: 13.5 us -> 0.03 us
  local copies, waits for them, and re-layouts: 0.21 us -> 3.55 us
    pallas_call x0 -> x2, Pallas kernels: none -> 323 us  [the longest x1 297 us: gather(): pl.pallas_call(functools.partial(gather_kernel, rows, cols, halves), out_...]
    psum x1 -> x0, waiting for transfers between devices: 50.1 us -> none  [broadcast(): return lax.psum(jnp.where(mine, x, jnp.zeros_like(x)), axis)]
    all_gather x1 -> x0, waiting for transfers between devices: 31.3 us -> none  [per_device(): columns = lax.all_gather(pair_elems, 'row', axis=0, tiled=True)]
    dot_general x1 -> x0, matrix products: 23.2 us -> none  [per_device(): lax.dot_general(scaled, columns, dims, preferred_element_type=jnp.float32)]
  transfers between devices with their start and end apart: 2 -> 0, of which waited for: 2 -> 0; matrix products, arithmetic and copies ran while one was open for 1% -> 0% of each run, Pallas kernels for 0% -> 0%
where the time goes in v1:
time: 330 us
  Pallas kernels  323 us (98%)
  local copies, waits for them, and re-layouts  3.55 us (1%)
    pallas_call x1, Pallas kernels, gather(): pl.pallas_call(functools.partial(gather_kernel, rows, cols, halves), out_...  297 us
    pallas_call x1, Pallas kernels, product(): pl.pallas_call(product_kernel, out_shape=jax.ShapeDtypeStruct((freqs, seg...  26.1 us

profile of v1, /device:TPU:3, one launch (start us, length us, event | category | flops | bytes accessed | tf_op | source)
XLA Modules:
  0.0 329.6 jit_solution(17653301666189469847)
XLA Ops:
  0.0 0.7 integer_pow.13
  0.7 0.9 select_reduce_fusion.1
  1.6 0.9 select_reduce_fusion
  2.6 0.7 broadcast_in_dim.26
  3.3 0.1 reshape.103
  3.4 0.2 add_divide_fusion.weights_ref
  3.6 297.2 %shard_map.73 = (bf16[8,40,3072]{2,1,0:T(8,128)(2,1)}, bf16[8,40,1536]{2,1,0:T(8,128)(2,1)}) custom-call(bf16[40,3072]{1,0:T(8,128)(2,1)} %x_ref.1), custom_call_target="tpu_custom_call" | custom-call | tf_op jit(solution)/shard_map/pallas_call | solution.py:213
  300.8 0.0 copy-start
  300.8 1.5 copy-done
  302.4 0.0 copy-start.1
  302.4 1.2 copy-done.1
  303.6 26.1 %shard_map.74 = f32[3,1536,3072]{2,1,0:T(8,128)} custom-call(f32[3,320,1]{2,1,0:T(8,128)S(1)} %add_divide_fusion.weights_ref, bf16[8,40,1536]{2,1,0:T(8,128)(2,1)S(1)} %copy-done.1, bf16[8,40,3072]{2,1,0:T(8,128)(2,1)S(1)} %copy-done), custom_call_target="tpu_custom_call" | custom-call | tf_op jit(solution)/shard_map/pallas_call | solution.py:253
  (1 shorter events, 0.0 us)
Async XLA Ops:
  300.8 1.5 copy-start
  302.4 1.2 copy-start.1

commit v2 on v1

v2 whole, which is shorter than its diff:
```python
import functools

import jax
import jax.numpy as jnp
from jax import lax
from jax.experimental import pallas as pl
from jax.experimental.pallas import tpu as pltpu
from jax.sharding import PartitionSpec as P

MESH = pl.DeviceIdType.MESH
LAG = 3


def ring_place(c, count):
    if count == 4:
        return c + (c // 2) * (1 - 2 * (c % 2))
    return c


def gather_kernel(rows, cols, halves, x_ref, cols_ref, seg_ref, own_sem, line_send, line_recv, mate_send, mate_recv,
                  enter_send, relay_send, ring_recv):
    r, c = lax.axis_index("row"), lax.axis_index("col")
    chips = rows // 2
    q, k = r // 2, r % 2
    pieces, lane = cols_ref.shape[1], cols_ref.shape[3]
    ratio = rows // cols
    chunks = ratio * halves
    place = ring_place(c, cols)
    source = r // ratio
    ring_next = [ring_place((place + 1) % cols, cols), ring_place((place + cols - 1) % cols, cols)]
    ahead = (place - ring_place(source, cols) + cols) % cols
    hops = [ahead, cols - ahead]
    up_ok, down_ok = q + 1 < chips, q >= 1

    own = [
        pltpu.make_async_copy(x_ref.at[:, pl.ds(p * lane, lane)], cols_ref.at[r, p], own_sem.at[p])
        for p in range(pieces)
    ]
    for copy in own:
        copy.start()
    barrier = pltpu.get_barrier_semaphore()

    def greet(row, col):
        pl.semaphore_signal(barrier, inc=1, device_id=(row, col), device_id_type=MESH)

    mate = 2 * q + 1 - k
    greet(mate, c)
    for nxt in ring_next:
        greet(2 * q, nxt)
        greet(2 * q + 1, nxt)

    @pl.when(up_ok)
    def _():
        greet(r + 2, c)

    @pl.when(down_ok)
    def _():
        greet(r - 2, c)

    pl.semaphore_wait(barrier, 5 + up_ok.astype(jnp.int32) + down_ok.astype(jnp.int32))
    for copy in own:
        copy.wait()

    def remote(src, dst, send, recv, row, col):
        return pltpu.make_async_remote_copy(
            src_ref=src, dst_ref=dst, send_sem=send, recv_sem=recv, device_id=(row, col), device_id_type=MESH
        )

    def block_of(stream, d, core):
        return 2 * (q - d if stream == 0 else q + d) + core

    def has(stream, d):
        return q >= d if stream == 0 else q + d < chips

    def line_copy(stream, d, j, b):
        ref = cols_ref.at[b, pl.ds(2 * j, 2)]
        row = r + 2 if stream == 0 else r - 2
        return remote(ref, ref, line_send.at[stream, d, j], line_recv.at[stream, d, j], row, c)

    def line_arrival(stream, d, j, b):
        ref = cols_ref.at[b, pl.ds(2 * j, 2)]
        return remote(ref, ref, line_send.at[stream, d, j], line_recv.at[stream, d - 1, j], mate, c)

    def mate_copy(b, j):
        ref = cols_ref.at[b, pl.ds(2 * j, 2)]
        return remote(ref, ref, mate_send.at[b, j], mate_recv.at[b, j], mate, c)

    def enter_copy(b, j, way):
        g = c * ratio + j // halves
        src = cols_ref.at[b, 2 * j + way]
        dst = seg_ref.at[b, 2 * (j % halves) + way]
        return remote(src, dst, enter_send.at[b, j, way], ring_recv.at[b, j % halves, way], g, ring_next[way])

    def relay_copy(b, j, way):
        ref = seg_ref.at[b, 2 * (j % halves) + way]
        return remote(ref, ref, relay_send.at[b, j % halves, way], ring_recv.at[b, j % halves, way], r, ring_next[way])

    def feeds(j):
        return (c * ratio + j // halves) // 2 == q

    def relays(j):
        return (source != c) & (j // halves == r % ratio)

    def onward(stream):
        return up_ok if stream == 0 else down_ok

    def line_part(step):
        d, j = step // chunks, step % chunks
        for stream in (0, 1):
            here = has(stream, d) if stream == 0 else has(stream, d) & (d > 0)
            b = block_of(stream, d, k)

            @pl.when(has(stream, d))
            def _():
                @pl.when(d > 0)
                def _():
                    line_arrival(stream, d, j, b).wait_recv()

                @pl.when(onward(stream))
                def _():
                    line_copy(stream, d, j, b).start()

            @pl.when(here)
            def _():
                mate_copy(b, j).start()

                @pl.when(feeds(j))
                def _():
                    for way in (0, 1):
                        enter_copy(b, j, way).start()

    def ring_part(step, way):
        d, j = step // chunks, step % chunks

        @pl.when(relays(j))
        def _():
            for stream in (0, 1):
                here = has(stream, d) if stream == 0 else has(stream, d) & (d > 0)

                @pl.when(here)
                def _():
                    for core in (0, 1):
                        b = block_of(stream, d, core)
                        relay_copy(b, j, way).wait_recv()

                        @pl.when(ring_next[way] != source)
                        def _():
                            relay_copy(b, j, way).start()

    steps = chunks * chips

    def body(step, carry):
        @pl.when(step < steps)
        def _():
            line_part(step)

        for way in (0, 1):
            late = step - LAG * hops[way]

            @pl.when((late >= 0) & (late < steps))
            def _():
                ring_part(late, way)

        return carry

    lax.fori_loop(0, steps + LAG * (cols - 1), body, 0)

    def finish(step, carry):
        d, j = step // chunks, step % chunks
        for stream in (0, 1):
            here = has(stream, d) if stream == 0 else has(stream, d) & (d > 0)
            b = block_of(stream, d, k)
            theirs = block_of(stream, d, 1 - k)

            @pl.when(has(stream, d) & onward(stream))
            def _():
                line_copy(stream, d, j, b).wait_send()

            @pl.when(here)
            def _():
                mate_copy(b, j).wait_send()
                mate_copy(theirs, j).wait_recv()

                @pl.when(feeds(j))
                def _():
                    for way in (0, 1):
                        enter_copy(b, j, way).wait_send()

                @pl.when(relays(j))
                def _():
                    for core in (0, 1):
                        e = block_of(stream, d, core)
                        for way in (0, 1):
                            @pl.when(ring_next[way] != source)
                            def _():
                                relay_copy(e, j, way).wait_send()

        return carry

    lax.fori_loop(0, steps, finish, 0)

    @pl.when(source == c)
    def _():
        here = pltpu.make_async_copy(cols_ref.at[:, pl.ds((r % ratio) * 2 * halves, 2 * halves)], seg_ref, own_sem.at[0])
        here.start()
        here.wait()


def gather(x, rows, cols):
    capacity, width = x.shape
    ratio = rows // cols
    seg_width = width // ratio
    halves = 2 if seg_width % 512 == 0 else 1
    chunks, chips = ratio * halves, rows // 2
    dma = pltpu.SemaphoreType.DMA
    return pl.pallas_call(
        functools.partial(gather_kernel, rows, cols, halves),
        out_shape=(
            jax.ShapeDtypeStruct((rows, 2 * chunks, capacity, seg_width // halves // 2), x.dtype),
            jax.ShapeDtypeStruct((rows, 2 * halves, capacity, seg_width // halves // 2), x.dtype),
        ),
        in_specs=[pl.BlockSpec(memory_space=pl.ANY)],
        out_specs=(pl.BlockSpec(memory_space=pltpu.VMEM), pl.BlockSpec(memory_space=pltpu.VMEM)),
        scratch_shapes=[
            dma((2 * chunks,)),
            dma((2, chips, chunks)),
            dma((2, chips, chunks)),
            dma((rows, chunks)),
            dma((rows, chunks)),
            dma((rows, chunks, 2)),
            dma((rows, halves, 2)),
            dma((rows, halves, 2)),
        ],
        compiler_params=pltpu.CompilerParams(collective_id=0, has_side_effects=True),
    )(x)


def exact_dot(a, b):
    return lax.dot_general(
        a, b, (((1,), (0,)), ((), ())), precision=lax.Precision.HIGHEST, preferred_element_type=jnp.float32
    )


def pick(band_ref, table_ref):
    levels, slots = table_ref.shape[1], band_ref.shape[1]
    hit = lax.broadcasted_iota(jnp.int32, (levels, slots), 0) == band_ref[...]
    return exact_dot(jnp.broadcast_to(table_ref[...], (8, levels)), hit.astype(jnp.float32))


def slot_target(counts_ref, shape, axis, capacity):
    slot = lax.broadcasted_iota(jnp.int32, shape, axis)
    target = jnp.full(shape, -1, jnp.int32)
    before = 0
    for block in range(counts_ref.shape[0]):
        inside = slot - block * capacity
        live = (inside >= 0) & (inside < counts_ref[block])
        target = jnp.where(live, inside + before, target)
        before = before + counts_ref[block]
    return target


def product_kernel(counts_ref, freq_ref, val_band, cond_band, val_energy, cond_energy, seg_ref, cols_ref, out_ref,
                   packed, turned, weights):
    which = pl.program_id(1)
    tile, (depth, width) = out_ref.shape[1], packed.shape
    rows, pieces, capacity, lane = cols_ref.shape
    slots = rows * capacity

    @pl.when((pl.program_id(0) == 0) & (which == 0))
    def _():
        place = slot_target(counts_ref, (1, slots), 1, capacity)
        choose = (lax.broadcasted_iota(jnp.int32, (depth, slots), 0) == place).astype(jnp.float32)
        gap = pick(cond_band, cond_energy) - pick(val_band, val_energy)
        gap = lax.dot_general(
            gap, choose, (((1,), (1,)), ((), ())), precision=lax.Precision.HIGHEST, preferred_element_type=jnp.float32
        )
        for f in range(weights.shape[0]):
            weights[f] = -4.0 * gap / (gap * gap + freq_ref[f] * freq_ref[f])
        choose = choose.astype(jnp.bfloat16)
        for p in range(pieces):
            piece = cols_ref[:, p].reshape(slots, lane)
            packed[:, p * lane : (p + 1) * lane] = jnp.dot(
                choose, piece, preferred_element_type=jnp.float32
            ).astype(jnp.bfloat16)
        for p in range(seg_ref.shape[1]):
            piece = seg_ref[:, p].reshape(slots, lane)
            turned[p * lane : (p + 1) * lane, :] = lax.dot_general(
                piece, choose, (((0,), (1,)), ((), ())), preferred_element_type=jnp.float32
            ).astype(jnp.bfloat16)

    start = pl.multiple_of(pl.program_id(0) * tile, tile)
    scaled = (turned[pl.ds(start, tile), :].astype(jnp.float32) * weights[which][:1]).astype(jnp.bfloat16)
    out_ref[0] = jnp.dot(scaled, packed[...], preferred_element_type=jnp.float32)


def product(counts, frequency, val_band, cond_band, val_energy, cond_energy, seg, columns):
    freqs = frequency.shape[0]
    rows, pieces, capacity, lane = columns.shape
    width, seg_width = pieces * lane, seg.shape[1] * lane
    slots = rows * capacity
    live = slots * 5 // 8
    depth = pl.cdiv(live, 256) * 256
    tile = 256
    smem, vmem = pl.BlockSpec(memory_space=pltpu.SMEM), pl.BlockSpec(memory_space=pltpu.VMEM)
    return pl.pallas_call(
        product_kernel,
        out_shape=jax.ShapeDtypeStruct((freqs, seg_width, width), jnp.float32),
        grid=(seg_width // tile, freqs),
        in_specs=[smem, smem, vmem, vmem, vmem, vmem, vmem, vmem],
        out_specs=pl.BlockSpec((1, tile, width), lambda m, f: (f, m, 0)),
        scratch_shapes=[
            pltpu.VMEM((depth, width), jnp.bfloat16),
            pltpu.VMEM((seg_width, depth), jnp.bfloat16),
            pltpu.VMEM((freqs, 8, depth), jnp.float32),
        ],
        compiler_params=pltpu.CompilerParams(vmem_limit_bytes=48 * 1024 * 1024),
    )(counts, frequency, val_band[None], cond_band[None], val_energy[None], cond_energy[None], seg, columns)


def per_device(pair_elems, counts, val_band, cond_band, val_energy, cond_energy, frequency):
    rows, cols = lax.axis_size("row"), lax.axis_size("col")
    columns, seg = gather(pair_elems, rows, cols)
    return product(counts, frequency, val_band, cond_band, val_energy, cond_energy, seg, columns)


def solution(mesh):
    in_specs = (P("row", "col"), P(), P(), P(), P(), P(), P())
    out_specs = P(None, "row", "col")
    return jax.shard_map(
        per_device, mesh=mesh, in_specs=in_specs, out_specs=out_specs, check_vma=False
    )
```

time: 330 us -> 64.6 us (0.20)
  Pallas kernels: 323 us -> 57.5 us
    pallas_call x1, Pallas kernels: 297 us -> 33.2 us  [gather(): pl.pallas_call(functools.partial(gather_kernel, rows, cols, halves), out_...]
where the time goes in v2:
time: 64.6 us; the launch traced here: 64.3 us
  Pallas kernels  57.5 us (89%)
  local copies, waits for them, and re-layouts  6.75 us (10%)
    pallas_call x1, Pallas kernels, gather(): pl.pallas_call(functools.partial(gather_kernel, rows, cols, halves), out_...  33.2 us
    pallas_call x1, Pallas kernels, product(): pl.pallas_call(product_kernel, out_shape=jax.ShapeDtypeStruct((freqs, seg...  24.3 us
    unnamed x12, local copies, waits for them, and re-layouts  5.38 us

profile of v2, /device:TPU:3, one launch (start us, length us, event | category | flops | bytes accessed | tf_op | source)
XLA Modules:
  0.0 64.3 jit_solution(18124554642261748761)
XLA Ops:
  0.0 0.7 %broadcast_in_dim.12.val_band = s32[1,320]{1,0:T(1,128)S(1)} reshape(s32[320]{0:T(512)} %param.9) | data formatting | bytes 2560 | tf_op jit(solution)/shard_map/broadcast_in_dim | solution.py:317
  0.7 0.7 %broadcast_in_dim.13.cond_band = s32[1,320]{1,0:T(1,128)S(1)} reshape(s32[320]{0:T(512)} %param.10) | data formatting | bytes 2560 | tf_op jit(solution)/shard_map/broadcast_in_dim | solution.py:317
  1.4 33.2 %shard_map.73 = (bf16[8,8,40,384]{3,2,1,0:T(8,128)(2,1)}, bf16[8,4,40,384]{3,2,1,0:T(8,128)(2,1)}) custom-call(bf16[40,3072]{1,0:T(8,128)(2,1)} %x_ref.1), custom_call_target="tpu_custom_call" | custom-call | tf_op jit(solution)/shard_map/pallas_call | solution.py:216
  34.6 0.0 copy-start
  34.6 1.5 %copy-done = bf16[8,8,40,384]{3,2,1,0:T(8,128)(2,1)S(1)} copy-done((bf16[8,8,40,384]{3,2,1,0:T(8,128)(2,1)S(1)}, bf16[8,8,40,384]{3,2,1,0:T(8,128)(2,1)}, u32[]{:S(2)}) %copy-start) | copy-done | bytes 1966104
  36.2 0.0 copy-start.1
  36.2 1.2 %copy-done.1 = bf16[8,4,40,384]{3,2,1,0:T(8,128)(2,1)S(1)} copy-done((bf16[8,4,40,384]{3,2,1,0:T(8,128)(2,1)S(1)}, bf16[8,4,40,384]{3,2,1,0:T(8,128)(2,1)}, u32[]{:S(2)}) %copy-start.1) | copy-done | bytes 983064
  37.4 0.0 copy-start.2
  37.4 0.7 %copy-done.2 = f32[512]{0:T(512)S(1)} copy-done((f32[512]{0:T(512)S(1)}, f32[512]{0:T(512)}, u32[]{:S(2)}) %copy-start.2) | copy-done | bytes 2072
  38.0 0.0 copy-start.3
  38.0 0.7 %copy-done.3 = s32[8]{0:T(128)S(1)} copy-done((s32[8]{0:T(128)S(1)}, s32[8]{0:T(128)}, u32[]{:S(2)}) %copy-start.3) | copy-done | bytes 56
  38.7 0.0 copy-start.4
  38.7 0.7 %copy-done.4 = f32[3]{0:T(128)S(1)} copy-done((f32[3]{0:T(128)S(1)}, f32[3]{0:T(128)}, u32[]{:S(2)}) %copy-start.4) | copy-done | bytes 36
  39.3 0.0 copy-start.5
  39.3 0.7 %copy-done.5 = f32[128]{0:T(128)S(1)} copy-done((f32[128]{0:T(128)S(1)}, f32[128]{0:T(128)}, u32[]{:S(2)}) %copy-start.5) | copy-done | bytes 536
  40.0 24.3 %shard_map.74 = f32[3,1536,3072]{2,1,0:T(8,128)} custom-call(s32[8]{0:T(128)S(1)} %copy-done.3, f32[3]{0:T(128)S(1)} %copy-done.4, s32[1,320]{1,0:T(1,128)S(1)} %broadcast_in_dim.12.val_band, s32[1,320]{1,0:T(1,128)S(1)} %broadcast_in_dim.13.cond_band, f32[1,128]{1,0:T(1,128)S(1)} %bitcast.3, f32[1,512]{1,0:T(1,128)S(1)} %bitcast.2, ...), custom_call_target="tpu_custom_call" | custom-call | tf_op jit(solution)/shard_map/pallas_call | solution.py:305
Async XLA Ops:
  34.6 1.5 %copy-start = (bf16[8,8,40,384]{3,2,1,0:T(8,128)(2,1)S(1)}, bf16[8,8,40,384]{3,2,1,0:T(8,128)(2,1)}, u32[]{:S(2)}) copy-start(bf16[8,8,40,384]{3,2,1,0:T(8,128)(2,1)} %get-tuple-element.8.cols_ref) | copy-start | bytes 5898244
  36.2 1.2 %copy-start.1 = (bf16[8,4,40,384]{3,2,1,0:T(8,128)(2,1)S(1)}, bf16[8,4,40,384]{3,2,1,0:T(8,128)(2,1)}, u32[]{:S(2)}) copy-start(bf16[8,4,40,384]{3,2,1,0:T(8,128)(2,1)} %get-tuple-element.7.seg_ref) | copy-start | bytes 2949124
  37.4 0.7 %copy-start.2 = (f32[512]{0:T(512)S(1)}, f32[512]{0:T(512)}, u32[]{:S(2)}) copy-start(f32[512]{0:T(512)} %param.12) | copy-start | bytes 6148
  38.0 0.7 %copy-start.3 = (s32[8]{0:T(128)S(1)}, s32[8]{0:T(128)}, u32[]{:S(2)}) copy-start(s32[8]{0:T(128)} %counts_ref.1) | copy-start | bytes 100
  38.7 0.7 %copy-start.4 = (f32[3]{0:T(128)S(1)}, f32[3]{0:T(128)}, u32[]{:S(2)}) copy-start(f32[3]{0:T(128)} %freq_ref.1) | copy-start | bytes 40
  39.3 0.7 %copy-start.5 = (f32[128]{0:T(128)S(1)}, f32[128]{0:T(128)}, u32[]{:S(2)}) copy-start(f32[128]{0:T(128)} %param.11) | copy-start | bytes 1540

commit v3 on v2

--- a/solution.py
+++ b/solution.py
@@ -1,4 +1,5 @@
 import functools
+import math
 
 import jax
 import jax.numpy as jnp
@@ -9,6 +10,7 @@
 
 MESH = pl.DeviceIdType.MESH
 LAG = 3
+TILE = 1024
 
 
 def ring_place(c, count):
@@ -17,8 +19,10 @@
     return c
 
 
-def gather_kernel(rows, cols, halves, x_ref, cols_ref, seg_ref, own_sem, line_send, line_recv, mate_send, mate_recv,
-                  enter_send, relay_send, ring_recv):
+def gather_kernel(rows, cols, halves, x_ref, counts_hbm, freq_hbm, val_band_hbm, cond_band_hbm, val_energy_hbm,
+                  cond_energy_hbm, cols_ref, seg_ref, choose_ref, weights_ref, counts_ref, freq_ref, val_band, cond_band,
+                  val_energy, cond_energy, small_sem, own_sem, line_send, line_recv, mate_send, mate_recv, enter_send,
+                  relay_send, ring_recv):
     r, c = lax.axis_index("row"), lax.axis_index("col")
     chips = rows // 2
     q, k = r // 2, r % 2
@@ -36,7 +40,14 @@
         pltpu.make_async_copy(x_ref.at[:, pl.ds(p * lane, lane)], cols_ref.at[r, p], own_sem.at[p])
         for p in range(pieces)
     ]
-    for copy in own:
+    small = [
+        pltpu.make_async_copy(src, dst, small_sem.at[i])
+        for i, (src, dst) in enumerate((
+            (counts_hbm, counts_ref), (freq_hbm, freq_ref), (val_band_hbm, val_band), (cond_band_hbm, cond_band),
+            (val_energy_hbm, val_energy), (cond_energy_hbm, cond_energy),
+        ))
+    ]
+    for copy in own + small:
         copy.start()
     barrier = pltpu.get_barrier_semaphore()
 
@@ -163,7 +174,20 @@
 
         return carry
 
-    lax.fori_loop(0, steps + LAG * (cols - 1), body, 0)
+    lax.fori_loop(0, chunks, body, 0)
+    for copy in small:
+        copy.wait()
+    capacity, (depth, slots) = x_ref.shape[0], choose_ref.shape
+    place_of = slot_target(counts_ref, (1, slots), 1, capacity)
+    choose = (lax.broadcasted_iota(jnp.int32, (depth, slots), 0) == place_of).astype(jnp.float32)
+    gap = pick(cond_band, cond_energy) - pick(val_band, val_energy)
+    gap = lax.dot_general(
+        gap, choose, (((1,), (1,)), ((), ())), precision=lax.Precision.HIGHEST, preferred_element_type=jnp.float32
+    )
+    for f in range(weights_ref.shape[0]):
+        weights_ref[f] = -4.0 * gap / (gap * gap + freq_ref[f] * freq_ref[f])
+    choose_ref[...] = choose.astype(jnp.bfloat16)
+    lax.fori_loop(chunks, steps + LAG * (cols - 1), body, 0)
 
     def finish(step, carry):
         d, j = step // chunks, step % chunks
@@ -206,8 +230,11 @@
         here.wait()
 
 
-def gather(x, rows, cols):
+def gather(x, counts, frequency, val_band, cond_band, val_energy, cond_energy, rows, cols):
     capacity, width = x.shape
+    slots = rows * capacity
+    live = slots * 5 // 8
+    depth = pl.cdiv(live, 256) * 256
     ratio = rows // cols
     seg_width = width // ratio
     halves = 2 if seg_width % 512 == 0 else 1
@@ -216,12 +243,21 @@
     return pl.pallas_call(
         functools.partial(gather_kernel, rows, cols, halves),
         out_shape=(
-            jax.ShapeDtypeStruct((rows, 2 * chunks, capacity, seg_width // halves // 2), x.dtype),
-            jax.ShapeDtypeStruct((rows, 2 * halves, capacity, seg_width // halves // 2), x.dtype),
+            pltpu.VMEM((rows, 2 * chunks, capacity, seg_width // halves // 2), x.dtype),
+            pltpu.VMEM((rows, 2 * halves, capacity, seg_width // halves // 2), x.dtype),
+            pltpu.VMEM((depth, slots), jnp.bfloat16),
+            pltpu.VMEM((frequency.shape[0], 8, depth), jnp.float32),
         ),
-        in_specs=[pl.BlockSpec(memory_space=pl.ANY)],
-        out_specs=(pl.BlockSpec(memory_space=pltpu.VMEM), pl.BlockSpec(memory_space=pltpu.VMEM)),
+        in_specs=[pl.BlockSpec(memory_space=pl.ANY)] * 7,
+        out_specs=[pl.BlockSpec(memory_space=pltpu.VMEM)] * 4,
         scratch_shapes=[
+            pltpu.SMEM(counts.shape, counts.dtype),
+            pltpu.SMEM(frequency.shape, frequency.dtype),
+            pltpu.VMEM(val_band.shape, val_band.dtype),
+            pltpu.VMEM(cond_band.shape, cond_band.dtype),
+            pltpu.VMEM(val_energy.shape, val_energy.dtype),
+            pltpu.VMEM(cond_energy.shape, cond_energy.dtype),
+            dma((6,)),
             dma((2 * chunks,)),
             dma((2, chips, chunks)),
             dma((2, chips, chunks)),
@@ -231,8 +267,10 @@
             dma((rows, halves, 2)),
             dma((rows, halves, 2)),
         ],
-        compiler_params=pltpu.CompilerParams(collective_id=0, has_side_effects=True),
-    )(x)
+        compiler_params=pltpu.CompilerParams(
+            collective_id=0, has_side_effects=True, vmem_limit_bytes=40 * 1024 * 1024
+        ),
+    )(x, counts, frequency, val_band, cond_band, val_energy, cond_energy)
 
 
 def exact_dot(a, b):
@@ -242,9 +280,9 @@
 
 
 def pick(band_ref, table_ref):
-    levels, slots = table_ref.shape[1], band_ref.shape[1]
-    hit = lax.broadcasted_iota(jnp.int32, (levels, slots), 0) == band_ref[...]
-    return exact_dot(jnp.broadcast_to(table_ref[...], (8, levels)), hit.astype(jnp.float32))
+    levels, slots = table_ref.shape[0], band_ref.shape[0]
+    hit = lax.broadcasted_iota(jnp.int32, (levels, slots), 0) == band_ref[...][None, :]
+    return exact_dot(jnp.broadcast_to(table_ref[...][None, :], (8, levels)), hit.astype(jnp.float32))
 
 
 def slot_target(counts_ref, shape, axis, capacity):
@@ -259,24 +297,15 @@
     return target
 
 
-def product_kernel(counts_ref, freq_ref, val_band, cond_band, val_energy, cond_energy, seg_ref, cols_ref, out_ref,
-                   packed, turned, weights):
-    which = pl.program_id(1)
-    tile, (depth, width) = out_ref.shape[1], packed.shape
+def product_kernel(weights, choose_ref, seg_ref, cols_ref, out_ref, packed, turned, scaled):
+    which, n = pl.program_id(0), pl.program_id(1)
+    tile = out_ref.shape[2]
     rows, pieces, capacity, lane = cols_ref.shape
     slots = rows * capacity
 
-    @pl.when((pl.program_id(0) == 0) & (which == 0))
-    def _():
-        place = slot_target(counts_ref, (1, slots), 1, capacity)
-        choose = (lax.broadcasted_iota(jnp.int32, (depth, slots), 0) == place).astype(jnp.float32)
-        gap = pick(cond_band, cond_energy) - pick(val_band, val_energy)
-        gap = lax.dot_general(
-            gap, choose, (((1,), (1,)), ((), ())), precision=lax.Precision.HIGHEST, preferred_element_type=jnp.float32
-        )
-        for f in range(weights.shape[0]):
-            weights[f] = -4.0 * gap / (gap * gap + freq_ref[f] * freq_ref[f])
-        choose = choose.astype(jnp.bfloat16)
+    @pl.when((n == 0) & (which == 0))
+    def _():
+        choose = choose_ref[...]
         for p in range(pieces):
             piece = cols_ref[:, p].reshape(slots, lane)
             packed[:, p * lane : (p + 1) * lane] = jnp.dot(
@@ -288,39 +317,42 @@
                 piece, choose, (((0,), (1,)), ((), ())), preferred_element_type=jnp.float32
             ).astype(jnp.bfloat16)
 
-    start = pl.multiple_of(pl.program_id(0) * tile, tile)
-    scaled = (turned[pl.ds(start, tile), :].astype(jnp.float32) * weights[which][:1]).astype(jnp.bfloat16)
-    out_ref[0] = jnp.dot(scaled, packed[...], preferred_element_type=jnp.float32)
-
-
-def product(counts, frequency, val_band, cond_band, val_energy, cond_energy, seg, columns):
-    freqs = frequency.shape[0]
+    @pl.when(n == 0)
+    def _():
+        scaled[...] = (turned[...].astype(jnp.float32) * weights[which][:1]).astype(jnp.bfloat16)
+
+    start = pl.multiple_of(n * tile, tile)
+    out_ref[0] = jnp.dot(scaled[...], packed[:, pl.ds(start, tile)], preferred_element_type=jnp.float32)
+
+
+def product(weights, choose, seg, columns):
+    freqs = weights.shape[0]
     rows, pieces, capacity, lane = columns.shape
     width, seg_width = pieces * lane, seg.shape[1] * lane
-    slots = rows * capacity
-    live = slots * 5 // 8
-    depth = pl.cdiv(live, 256) * 256
-    tile = 256
-    smem, vmem = pl.BlockSpec(memory_space=pltpu.SMEM), pl.BlockSpec(memory_space=pltpu.VMEM)
+    depth = choose.shape[0]
+    tile = math.gcd(width, TILE)
+    vmem = pl.BlockSpec(memory_space=pltpu.VMEM)
     return pl.pallas_call(
         product_kernel,
         out_shape=jax.ShapeDtypeStruct((freqs, seg_width, width), jnp.float32),
-        grid=(seg_width // tile, freqs),
-        in_specs=[smem, smem, vmem, vmem, vmem, vmem, vmem, vmem],
-        out_specs=pl.BlockSpec((1, tile, width), lambda m, f: (f, m, 0)),
+        grid=(freqs, width // tile),
+        in_specs=[vmem] * 4,
+        out_specs=pl.BlockSpec((1, seg_width, tile), lambda f, n: (f, 0, n)),
         scratch_shapes=[
             pltpu.VMEM((depth, width), jnp.bfloat16),
             pltpu.VMEM((seg_width, depth), jnp.bfloat16),
-            pltpu.VMEM((freqs, 8, depth), jnp.float32),
+            pltpu.VMEM((seg_width, depth), jnp.bfloat16),
         ],
-        compiler_params=pltpu.CompilerParams(vmem_limit_bytes=48 * 1024 * 1024),
-    )(counts, frequency, val_band[None], cond_band[None], val_energy[None], cond_energy[None], seg, columns)
+        compiler_params=pltpu.CompilerParams(vmem_limit_bytes=40 * 1024 * 1024),
+    )(weights, choose, seg, columns)
 
 
 def per_device(pair_elems, counts, val_band, cond_band, val_energy, cond_energy, frequency):
     rows, cols = lax.axis_size("row"), lax.axis_size("col")
-    columns, seg = gather(pair_elems, rows, cols)
-    return product(counts, frequency, val_band, cond_band, val_energy, cond_energy, seg, columns)
+    columns, seg, choose, weights = gather(
+        pair_elems, counts, frequency, val_band, cond_band, val_energy, cond_energy, rows, cols
+    )
+    return product(weights, choose, seg, columns)
 
 
 def solution(mesh):

time: 64.6 us -> 57.8 us (0.89)
  Pallas kernels: 57.5 us -> 52.6 us
  local copies, waits for them, and re-layouts: 6.75 us -> 4.95 us
    pallas_call x1, Pallas kernels: 24.3 us -> 20.8 us  [product(): pl.pallas_call(product_kernel, out_shape=jax.ShapeDtypeStruct((freqs, seg...]
    pallas_call x1, Pallas kernels: 33.2 us -> 31.8 us  [gather(): pl.pallas_call(functools.partial(gather_kernel, rows, cols, halves), out_...]
    broadcast_in_dim x2 -> x0, local copies, waits for them, and re-layouts: 1.37 us -> none  [the longest x1 0.68 us: product(): val_band[None]]
    unnamed x12 -> x14, local copies, waits for them, and re-layouts: 5.38 us -> 4.95 us
where the time goes in v3:
time: 57.8 us; the launch traced here: 57.5 us
  Pallas kernels  52.6 us (91%)
  local copies, waits for them, and re-layouts  4.95 us (9%)
    pallas_call x1, Pallas kernels, gather(): pl.pallas_call(functools.partial(gather_kernel, rows, cols, halves), out_...  31.8 us
    pallas_call x1, Pallas kernels, product(): pl.pallas_call(product_kernel, out_shape=jax.ShapeDtypeStruct((freqs, seg...  20.8 us
    unnamed x14, local copies, waits for them, and re-layouts  4.95 us

profile of v3, /device:TPU:3, one launch (start us, length us, event | category | flops | bytes accessed | tf_op | source)
XLA Modules:
  0.0 57.5 jit_solution(3632057019535420808)
XLA Ops:
  0.0 0.0 copy-start
  0.0 0.9 %copy-done = bf16[40,3072]{1,0:T(8,128)(2,1)S(1)} copy-done((bf16[40,3072]{1,0:T(8,128)(2,1)S(1)}, bf16[40,3072]{1,0:T(8,128)(2,1)}, u32[]{:S(2)}) %copy-start) | copy-done | bytes 245784
  0.9 0.0 copy-start.1
  0.9 0.7 %copy-done.1 = s32[320]{0:T(512)S(1)} copy-done((s32[320]{0:T(512)S(1)}, s32[320]{0:T(512)}, u32[]{:S(2)}) %copy-start.1) | copy-done | bytes 1304
  1.6 0.0 copy-start.2
  1.6 0.7 %copy-done.2 = s32[320]{0:T(512)S(1)} copy-done((s32[320]{0:T(512)S(1)}, s32[320]{0:T(512)}, u32[]{:S(2)}) %copy-start.2) | copy-done | bytes 1304
  2.3 0.0 copy-start.3
  2.3 0.7 %copy-done.3 = f32[512]{0:T(512)S(1)} copy-done((f32[512]{0:T(512)S(1)}, f32[512]{0:T(512)}, u32[]{:S(2)}) %copy-start.3) | copy-done | bytes 2072
  3.0 0.0 copy-start.4
  3.0 0.7 %copy-done.4 = s32[8]{0:T(128)S(1)} copy-done((s32[8]{0:T(128)S(1)}, s32[8]{0:T(128)}, u32[]{:S(2)}) %copy-start.4) | copy-done | bytes 56
  3.6 0.0 copy-start.5
  3.6 0.7 %copy-done.5 = f32[3]{0:T(128)S(1)} copy-done((f32[3]{0:T(128)S(1)}, f32[3]{0:T(128)}, u32[]{:S(2)}) %copy-start.5) | copy-done | bytes 36
  4.3 0.0 copy-start.6
  4.3 0.7 %copy-done.6 = f32[128]{0:T(128)S(1)} copy-done((f32[128]{0:T(128)S(1)}, f32[128]{0:T(128)}, u32[]{:S(2)}) %copy-start.6) | copy-done | bytes 536
  5.0 31.8 %shard_map.73 = (bf16[8,8,40,384]{3,2,1,0:T(8,128)(2,1)S(1)}, bf16[8,4,40,384]{3,2,1,0:T(8,128)(2,1)S(1)}, bf16[256,320]{1,0:T(8,128)(2,1)S(1)}, f32[3,8,256]{2,1,0:T(8,128)S(1)}) custom-call(bf16[40,3072]{1,0:T(8,128)(2,1)S(1)} %copy-done, s32[8]{0:T(128)S(1)} %copy-done.4, f32[3]{0:T(128)S(1)} %copy-done.5, s32[320]{0:T(512)S(1)} %copy-done.1, ...), custom_call_target="tpu_custom_call" | custom-call | tf_op jit(solution)/shard_map/pallas_call | solution.py:243
  36.7 20.8 %shard_map.74 = f32[3,1536,3072]{2,1,0:T(8,128)} custom-call(f32[3,8,256]{2,1,0:T(8,128)S(1)} %get-tuple-element.9.weights, bf16[256,320]{1,0:T(8,128)(2,1)S(1)} %get-tuple-element.10.choose_ref, bf16[8,4,40,384]{3,2,1,0:T(8,128)(2,1)S(1)} %get-tuple-element.11.seg_ref, bf16[8,8,40,384]{3,2,1,0:T(8,128)(2,1)S(1)} %get-tuple-element.12.cols_ref), custom_call_target="tpu_custom_call" | custom-call | tf_op jit(solution)/shard_map/pallas_call | solution.py:335
Async XLA Ops:
  0.0 0.9 %copy-start = (bf16[40,3072]{1,0:T(8,128)(2,1)S(1)}, bf16[40,3072]{1,0:T(8,128)(2,1)}, u32[]{:S(2)}) copy-start(bf16[40,3072]{1,0:T(8,128)(2,1)} %x_ref.1) | copy-start | bytes 737284
  0.9 0.7 %copy-start.1 = (s32[320]{0:T(512)S(1)}, s32[320]{0:T(512)}, u32[]{:S(2)}) copy-start(s32[320]{0:T(512)} %val_band_hbm.1) | copy-start | bytes 3844
  1.6 0.7 %copy-start.2 = (s32[320]{0:T(512)S(1)}, s32[320]{0:T(512)}, u32[]{:S(2)}) copy-start(s32[320]{0:T(512)} %cond_band_hbm.1) | copy-start | bytes 3844
  2.3 0.7 %copy-start.3 = (f32[512]{0:T(512)S(1)}, f32[512]{0:T(512)}, u32[]{:S(2)}) copy-start(f32[512]{0:T(512)} %cond_energy_hbm.1) | copy-start | bytes 6148
  3.0 0.7 %copy-start.4 = (s32[8]{0:T(128)S(1)}, s32[8]{0:T(128)}, u32[]{:S(2)}) copy-start(s32[8]{0:T(128)} %counts_hbm.1) | copy-start | bytes 100
  3.6 0.7 %copy-start.5 = (f32[3]{0:T(128)S(1)}, f32[3]{0:T(128)}, u32[]{:S(2)}) copy-start(f32[3]{0:T(128)} %freq_hbm.1) | copy-start | bytes 40
  4.3 0.7 %copy-start.6 = (f32[128]{0:T(128)S(1)}, f32[128]{0:T(128)}, u32[]{:S(2)}) copy-start(f32[128]{0:T(128)} %val_energy_hbm.1) | copy-start | bytes 1540
